TPU v7x, 32 devices: a whole 2x2x4 slice. The times are simulated.
32 devices in a mesh: row: 4 (over y, x), col: 8 (over z, core).
Axes of the slice: x: 2, y: 2, z: 4, core: 2. Of those that a mesh axis runs over, the one named last changes fastest.
Arguments:
- activations: bfloat16 [256, 16384], P(None, 'row'), may hold values from -3 to 3
- cotangent: bfloat16 [256, 16384], P(None, 'row'), may hold values from -0.59765625 to 0.59765625
- forget: int32 [256], replicated, may hold values 0 or 1
- lengths: int32 [4, 4], P('row'), may hold values from 1 to 32, 64 in all within a row
- query_weight: bfloat16 [16384, 8192], P('row', 'col'), may hold values from -0.046875 to 0.046875
- key_weight: bfloat16 [16384, 512], P('row'), may hold values from -0.046875 to 0.046875
- value_weight: bfloat16 [16384, 512], P('row'), may hold values from -0.046875 to 0.046875
- output_projection_weight: bfloat16 [8192, 16384], P('col', 'row'), may hold values from -0.0625 to 0.0625
- query_down: bfloat16 [16384, 32], P('row'), may hold values from -0.046875 to 0.046875
- query_up: bfloat16 [32, 8192], P(None, 'col'), may hold values from -1 to 1
- output_down: bfloat16 [8192, 32], P('col'), may hold values from -0.0625 to 0.0625
- output_up: bfloat16 [32, 16384], P(None, 'row'), may hold values from -1 to 1
Outputs:
- query_down_gradient: float32 [16384, 32], P('row')
- query_up_gradient: float32 [32, 8192], P(None, 'col')
- output_down_gradient: float32 [8192, 32], P('col')
- output_up_gradient: float32 [32, 16384], P(None, 'row')
Inputs may be any that keep to these rules, and one draw needn't show every extreme that they name: In every row of lengths the 4 values sum to 64, and the largest is exactly 32.
All inputs are finite; a program needn't handle non-finite values.
Results may differ from a plain program's by a relative error of at most 0.025.
Values may be sent and summed in bfloat16 or wider, within the bound.
A program may use at most 128 MiB of HBM per device.

v0:
```python
import math
import jax
import jax.numpy as jnp
from jax import lax
from jax.sharding import PartitionSpec as P

HD = 128
HEADS = 64
KVH = 4
adapter_scale = 0.5
highest_precision = lax.Precision.HIGHEST


def row_contraction(left, right):
    return lax.dot_general(
        left, right, (((1,), (1,)), ((), ())), preferred_element_type=jnp.float32
    )


def token_contraction(left, right):
    return lax.dot_general(
        left, right, (((0,), (0,)), ((), ())), preferred_element_type=jnp.float32
    )


def local(
    activations,
    cotangent,
    forget,
    lengths,
    query_weight,
    key_weight,
    value_weight,
    output_projection_weight,
    query_down,
    query_up,
    output_down,
    output_up,
):
    row_index = lax.axis_index("row")
    col_index = lax.axis_index("col")
    tok_blk = activations.shape[0] // lax.axis_size("row")
    query_cols = query_weight.shape[1]
    heads_dev = query_cols // HD
    group_index = col_index * heads_dev // (HEADS // KVH)
    inverse = 1.0 / math.sqrt(HD)
    up_projection_broad = query_up.astype(jnp.float32)
    down_projection_broad = output_down.astype(jnp.float32)
    key_slice = lax.dynamic_slice_in_dim(key_weight, group_index * HD, HD, 1)
    value_slice = lax.dynamic_slice_in_dim(value_weight, group_index * HD, HD, 1)
    kv_cols = key_slice.shape[1]
    block_of_rows = activations
    reduced_result = jnp.dot(block_of_rows, query_down, preferred_element_type=jnp.float32)
    query_partial_term = jnp.dot(block_of_rows, query_weight, preferred_element_type=jnp.float32)
    query_partial_term = query_partial_term + adapter_scale * jnp.dot(
        reduced_result, up_projection_broad, precision=highest_precision
    )
    key_term = jnp.dot(block_of_rows, key_slice, preferred_element_type=jnp.float32)
    value_term = jnp.dot(block_of_rows, value_slice, preferred_element_type=jnp.float32)
    summed = lax.psum_scatter(
        jnp.concatenate([query_partial_term, key_term, value_term, reduced_result], axis=1).astype(
            jnp.bfloat16
        ),
        "row",
        scatter_dimension=0,
        tiled=True,
    ).astype(jnp.float32)
    query_heads = summed[:, :query_cols].astype(jnp.bfloat16).reshape(tok_blk, heads_dev, HD)
    key_part = summed[:, query_cols : query_cols + kv_cols].astype(jnp.bfloat16)
    value_part = summed[:, query_cols + kv_cols : query_cols + 2 * kv_cols].astype(jnp.bfloat16)
    input_lowrank_factor = summed[:, query_cols + 2 * kv_cols :]
    seg_ends = jnp.cumsum(lengths[0])
    position = jnp.arange(tok_blk, dtype=jnp.int32)
    segment = jnp.sum((position[:, None] >= seg_ends[None, :]).astype(jnp.int32), axis=1)
    allowed = (segment[:, None] == segment[None, :]) & (position[None, :] <= position[:, None])
    scores = (
        jnp.einsum("qhd,kd->hqk", query_heads, key_part, preferred_element_type=jnp.float32)
        * inverse
    )
    numerator = jnp.where(allowed[None], jnp.exp(scores), 0.0)
    softmax = numerator / jnp.sum(numerator, axis=2, keepdims=True)
    weights = softmax.astype(jnp.bfloat16)
    hidden_state = jnp.einsum(
        "hqk,kd->qhd", weights, value_part, preferred_element_type=jnp.float32
    )
    hidden_state = hidden_state.reshape(tok_blk, query_cols).astype(jnp.bfloat16)
    sign_flip = (1 - 2 * forget).astype(jnp.bfloat16)
    output_gradient = cotangent * sign_flip[:, None]
    block_of_rows = output_gradient
    reduced_result = row_contraction(block_of_rows, output_up)
    hidden_state_term = row_contraction(
        block_of_rows, output_projection_weight
    ) + adapter_scale * jnp.dot(
        reduced_result, down_projection_broad.T, precision=highest_precision
    )
    backward = lax.psum_scatter(
        jnp.concatenate([hidden_state_term, reduced_result], axis=1).astype(jnp.bfloat16),
        "row",
        scatter_dimension=0,
        tiled=True,
    ).astype(jnp.float32)
    hidden_grad = backward[:, :query_cols].astype(jnp.bfloat16).reshape(tok_blk, heads_dev, HD)
    gradient_lowrank_factor = backward[:, query_cols:]
    prob_grad = jnp.einsum(
        "qhd,kd->hqk", hidden_grad, value_part, preferred_element_type=jnp.float32
    )
    score_grad = softmax * (prob_grad - jnp.sum(prob_grad * softmax, axis=2, keepdims=True))
    query_gradient = (
        jnp.einsum(
            "hqk,kd->qhd", score_grad, key_part.astype(jnp.float32), precision=highest_precision
        )
        * inverse
    )
    query_gradient = query_gradient.reshape(tok_blk, query_cols)
    query_lowrank_factor = jnp.dot(
        query_gradient, up_projection_broad.T, precision=highest_precision
    )
    hidden_state_factor = jnp.dot(hidden_state, output_down, preferred_element_type=jnp.float32)
    up_projection_piece = adapter_scale * jnp.dot(
        input_lowrank_factor.T, query_gradient, precision=highest_precision
    )
    down_projection_piece = adapter_scale * jnp.dot(
        hidden_state.astype(jnp.float32).T, gradient_lowrank_factor, precision=highest_precision
    )
    query_up_gradient, output_down_gradient = (
        lax.psum(up_projection_piece.astype(jnp.bfloat16), "row").astype(jnp.float32),
        lax.psum(down_projection_piece.astype(jnp.bfloat16), "row").astype(jnp.float32),
    )
    zero_rows = jnp.zeros((activations.shape[0], query_lowrank_factor.shape[1]), jnp.float32)
    first_token = row_index * tok_blk
    query_padded = lax.dynamic_update_slice_in_dim(zero_rows, query_lowrank_factor, first_token, 0)
    hidden_padded = lax.dynamic_update_slice_in_dim(zero_rows, hidden_state_factor, first_token, 0)
    query_total, hidden_total = lax.psum((query_padded, hidden_padded), ("row", "col"))
    query_everywhere = query_total.astype(jnp.bfloat16)
    hidden_state_everywhere = hidden_total.astype(jnp.bfloat16)
    query_down_gradient = adapter_scale * token_contraction(activations, query_everywhere)
    output_up_gradient = adapter_scale * token_contraction(hidden_state_everywhere, output_gradient)
    return (query_down_gradient, query_up_gradient, output_down_gradient, output_up_gradient)


def solution(mesh):
    placed = (
        P(None, "row"),
        P(None, "row"),
        P(),
        P("row", None),
        P("row", "col"),
        P("row", None),
        P("row", None),
        P("col", "row"),
        P("row", None),
        P(None, "col"),
        P("col", None),
        P(None, "row"),
    )
    return jax.shard_map(
        local,
        mesh=mesh,
        in_specs=placed,
        out_specs=(P("row", None), P(None, "col"), P("col", None), P(None, "row")),
        check_vma=False,
    )
```

profile of v0, /device:TPU:0, one launch (start us, length us, event | category | flops | bytes accessed | tf_op | source)
XLA Modules:
  0.0 180.6 jit_solution(12886477900674417634)
XLA Ops:
  7.2 0.0 copy-start
  7.2 0.0 reduce-scatter.3.cloned.1.call-start
  7.2 1.5 copy-done
  8.8 1.7 fusion.58
  10.5 0.1 copy.46
  10.6 1.9 %fusion.17 = bf16[256,128]{1,0:T(8,128)(2,1)S(1)} fusion(bf16[256,4096]{1,0:T(8,128)(2,1)S(1)} %copy-done, bf16[4096,512]{1,0:T(8,128)(2,1)} %param.17, s32[]{:T(128)S(6)} %select_n.18), kind=kOutput, calls=%fused_computation.29 | convolution fusion | flops 268468224 | bytes 3211268 | tf_op jit(solution)/shard_map/dot_general | solution.py:58
  12.5 1.9 %fusion.18 = bf16[256,128]{1,0:T(8,128)(2,1)S(1)} fusion(bf16[256,4096]{1,0:T(8,128)(2,1)S(1)} %copy-done, bf16[4096,512]{1,0:T(8,128)(2,1)} %param.18, s32[]{:T(128)S(6)} %select_n.18), kind=kOutput, calls=%fused_computation.30 | convolution fusion | flops 268468224 | bytes 3211268 | tf_op jit(solution)/shard_map/dot_general | solution.py:59
  14.4 0.0 copy-start.1
  14.4 5.7 %fusion.60 = f32[256,1024]{1,0:T(8,128)S(1)} fusion(bf16[256,4096]{1,0:T(8,128)(2,1)S(1)} %copy-done, bf16[4096,1024]{1,0:T(8,128)(2,1)} %param.16), kind=kOutput, calls=%fused_computation.79 | convolution fusion | flops 2147483648 | bytes 11534336 | tf_op jit(solution)/shard_map/dot_general | solution.py:54
  20.2 0.0 copy-start.4
  20.2 0.0 copy-start.3
  20.2 0.0 copy-done.1
  20.2 0.7 fusion.8
  20.9 0.9 pad_maximum_fusion
  21.8 0.0 reduce-scatter.3.cloned.1.call-update
  21.8 0.0 reduce-scatter.5.cloned.1.call-start
  21.9 2.4 %fusion.59 = (bf16[256,32]{0,1:T(8,128)(2,1)S(1)}, f32[256,32]{0,1:T(8,128)S(1)}) fusion(bf16[32,4096]{1,0:T(8,128)(2,1)S(1)} %copy-done.3, bf16[256,4096]{1,0:T(8,128)(2,1)} %param.13, bf16[256]{0:T(256)(128)(2,1)S(1)} %subtract_convert_fusion), kind=kOutput, calls=%fused_computation.78 | convolution fusion | flops 68165632 | bytes 2408960 | tf_op jit(solution)/shard_map/dot_general | solution.py:15
  24.3 0.1 copy.48
  24.5 0.0 copy-start.2
  24.5 6.4 %fusion.4 = f32[256,1024]{1,0:T(8,128)S(1)} fusion(bf16[1024,4096]{1,0:T(8,128)(2,1)} %param.19, bf16[256,4096]{1,0:T(8,128)(2,1)} %param.13, bf16[256]{0:T(256)(128)(2,1)S(1)} %subtract_convert_fusion), kind=kOutput, calls=%fused_computation.6 | convolution fusion | flops 2148532224 | bytes 11534848 | tf_op jit(solution)/shard_map/dot_general | solution.py:15
  30.9 0.0 copy-start.5
  30.9 0.0 copy-done.2
  30.9 0.6 fusion.9
  31.5 0.9 pad_maximum_fusion.1
  32.4 0.0 reduce-scatter.5.cloned.1.call-update
  32.4 0.0 all-reduce.4.cloned.1.call-start
  32.5 0.2 reduce-window.8
  32.7 0.1 convert_reduce_fusion
  32.8 0.1 fusion.44
  32.8 17.6 %reduce-scatter.3.cloned.1.call-done = bf16[64,1312]{1,0:T(8,128)(2,1)} async-done(((bf16[256,1312]{1,0:T(8,128)(2,1)}), bf16[64,1312]{1,0:T(8,128)(2,1)}) %reduce-scatter.3.cloned.1.call-update) | async-done | bytes 167952 | tf_op jit(solution)/shard_map/reduce_scatter | solution.py:60
  50.4 1.2 fusion.41
  51.7 0.9 fusion.14
  52.6 0.1 fusion.31
  52.7 25.9 %reduce-scatter.5.cloned.1.call-done = bf16[64,1056]{1,0:T(8,128)(2,1)} async-done(((bf16[256,1056]{1,0:T(8,128)(2,1)}), bf16[64,1056]{1,0:T(8,128)(2,1)}) %reduce-scatter.5.cloned.1.call-update) | async-done | bytes 135184 | tf_op jit(solution)/shard_map/reduce_scatter | solution.py:96
  78.7 1.2 multiply_reduce_fusion
  79.8 1.1 fusion.10
  81.0 0.3 fusion.25
  81.2 0.3 dynamic_update_slice.7
  81.6 0.3 dynamic_update_slice.6
  82.0 39.9 %all-reduce = (bf16[256,32]{0,1:T(8,128)(2,1)S(1)}, bf16[256,32]{0,1:T(8,128)(2,1)S(1)}) all-reduce(f32[256,32]{0,1:T(8,128)S(1)} %dynamic_update_slice.6, f32[256,32]{0,1:T(8,128)S(1)} %dynamic_update_slice.7), channel_id=1, replica_groups=mesh['row'=4,'col'=8] {'row','col'}, use_global_device_ids=true, to_apply=%region_6.7 | all-reduce | flops 16384 | bytes 98304 | tf_op jit(solution)/shard_map/psum | solution.py:133
  121.9 2.9 %convolution_multiply_fusion = f32[32,4096]{1,0:T(8,128)} fusion(bf16[256,4096]{1,0:T(8,128)(2,1)} %param.13, bf16[256]{0:T(256)(128)(2,1)S(1)} %subtract_convert_fusion, bf16[256,32]{0,1:T(8,128)(2,1)S(1)} %get-tuple-element.5), kind=kOutput, calls=%fused_computation | convolution fusion | flops 68288512 | bytes 2638336 | tf_op jit(solution)/shard_map/dot_general | solution.py:21
  124.8 1.6 fusion.16
  126.4 1.6 fusion.15
  128.0 0.0 all-reduce.4.cloned.1.call-update
  128.0 1.3 fusion
  129.2 41.8 %all-reduce.4.cloned.1.call-done = (bf16[32,1024]{1,0:T(8,128)(2,1)}, bf16[1024,32]{0,1:T(8,128)(2,1)}) async-done(((bf16[32,1024]{1,0:T(8,128)(2,1)}, bf16[1024,32]{0,1:T(8,128)(2,1)}), (bf16[32,1024]{1,0:T(8,128)(2,1)}, bf16[1024,32]{0,1:T(8,128)(2,1)})) %all-reduce.4.cloned.1.call-update) | async-done | bytes 131088 | tf_op jit(solution)/shard_map/psum | solution.py:126
  171.0 1.5 convert_element_type.52
  172.5 1.5 convert_element_type.58
  (6 shorter events, 0.0 us)
Async XLA Ops:
  7.2 1.6 copy-start
  7.2 43.3 %reduce-scatter.3.cloned.1.call-start = ((), (), s32[]{:S(2)}) async-start(), calls=%async_computation.2 | async-start | bytes 901120 | tf_op jit(solution)/shard_map/reduce_scatter | solution.py:60
  14.4 5.8 %copy-start.1 = (bf16[32,1024]{1,0:T(8,128)(2,1)S(1)}, bf16[32,1024]{1,0:T(8,128)(2,1)}, u32[]{:S(2)}) copy-start(bf16[32,1024]{1,0:T(8,128)(2,1)} %param.21) | copy-start | bytes 196612
  20.2 1.7 copy-start.4
  20.2 1.7 copy-start.3
  21.8 56.8 %reduce-scatter.5.cloned.1.call-start = ((), (), s32[]{:S(2)}) async-start(), calls=%async_computation.3 | async-start | bytes 737280 | tf_op jit(solution)/shard_map/reduce_scatter | solution.py:96
  24.5 6.4 %copy-start.2 = (bf16[1024,32]{0,1:T(8,128)(2,1)S(1)}, bf16[1024,32]{0,1:T(8,128)(2,1)}, u32[]{:S(2)}) copy-start(bf16[1024,32]{0,1:T(8,128)(2,1)} %param.22) | copy-start | bytes 196612
  30.9 1.6 copy-start.5
  32.4 138.6 %all-reduce.4.cloned.1.call-start = ((), (), s32[]{:S(2)}) async-start(), calls=%async_computation.4 | async-start | bytes 262144 | tf_op jit(solution)/shard_map/psum | solution.py:126
Sparse Core Ops, SparseCore 0:
  22.0 28.4 reduce-scatter.2
  53.6 25.0 reduce-scatter.4
  128.1 42.8 all-reduce.3
where the time goes:
time: 181 us
  waiting for transfers between devices  85.3 us (47%)
  blocking collectives  39.9 us (22%)
  matrix products  33.5 us (19%)
  between operations  14 us (8%)
  other arithmetic  5.14 us (3%)
  local copies, waits for them, and re-layouts  2.51 us (1%)
    psum x1, waiting for transfers between devices, local(): lax.psum(up_projection_piece.astype(jnp.bfloat16), 'row')  41.8 us
    psum x1, blocking collectives, local(): lax.psum((query_padded, hidden_padded), ('row', 'col'))  39.9 us
    reduce_scatter x1, waiting for transfers between devices, local(): lax.psum_scatter(jnp.concatenate([hidden_state_term, reduced_result], axi...  25.9 us
    reduce_scatter x1, waiting for transfers between devices, local(): lax.psum_scatter(jnp.concatenate([query_partial_term, key_term, value_ter...  17.6 us
    dot_general x2, matrix products, row_contraction(): lax.dot_general(left, right, (((1,), (1,)), ((), ())), preferred_element_...  8.79 us
    dot_general x1, matrix products, local(): jnp.dot(block_of_rows, query_weight, preferred_element_type=jnp.float32)  5.74 us
    dot_general x2, matrix products, token_contraction(): lax.dot_general(left, right, (((0,), (0,)), ((), ())), preferred_element_...  4.2 us
  transfers between devices with their start and end apart: 3, of which 3 were waited for; matrix products, arithmetic and copies ran while one was open for 8% of the time, Pallas kernels for 0%

commit v1 on v0

--- a/solution.py
+++ b/solution.py
@@ -9,6 +9,11 @@
 KVH = 4
 adapter_scale = 0.5
 highest_precision = lax.Precision.HIGHEST
+
+
+def by_each_axis(array, first, second):
+    partial = lax.psum(array, first)
+    return lax.psum(partial, second)
 
 
 def row_contraction(left, right):
@@ -130,7 +135,7 @@
     first_token = row_index * tok_blk
     query_padded = lax.dynamic_update_slice_in_dim(zero_rows, query_lowrank_factor, first_token, 0)
     hidden_padded = lax.dynamic_update_slice_in_dim(zero_rows, hidden_state_factor, first_token, 0)
-    query_total, hidden_total = lax.psum((query_padded, hidden_padded), ("row", "col"))
+    query_total, hidden_total = by_each_axis((query_padded, hidden_padded), "col", "row")
     query_everywhere = query_total.astype(jnp.bfloat16)
     hidden_state_everywhere = hidden_total.astype(jnp.bfloat16)
     query_down_gradient = adapter_scale * token_contraction(activations, query_everywhere)

time: 181 us -> 192 us (1.061)
  waiting for transfers between devices: 85.3 us -> 118 us
  blocking collectives: 39.9 us -> 17.5 us
    psum x0 -> x1, waiting for transfers between devices: none -> 50.9 us  [by_each_axis(): partial = lax.psum(array, first)]
    psum x1, blocking collectives: 39.9 us -> 17.5 us  [by_each_axis(): return lax.psum(partial, second)]
    psum x1, waiting for transfers between devices: 41.8 us -> 23.1 us  [local(): lax.psum(up_projection_piece.astype(jnp.bfloat16), 'row')]
  transfers between devices with their start and end apart: 3 -> 4, of which waited for: 3 -> 4; matrix products, arithmetic and copies ran while one was open for 8% -> 11% of each run, Pallas kernels for 0% -> 0%
where the time goes in v1:
time: 192 us; the launch traced here: 191 us
  waiting for transfers between devices  118 us (61%)
  matrix products  33.5 us (17%)
  blocking collectives  17.5 us (9%)
  between operations  14 us (7%)
  other arithmetic  5.16 us (3%)
  local copies, waits for them, and re-layouts  3.13 us (2%)
    psum x1, waiting for transfers between devices, by_each_axis(): partial = lax.psum(array, first)  50.9 us
    reduce_scatter x1, waiting for transfers between devices, local(): lax.psum_scatter(jnp.concatenate([hidden_state_term, reduced_result], axi...  25.9 us
    psum x1, waiting for transfers between devices, local(): lax.psum(up_projection_piece.astype(jnp.bfloat16), 'row')  23.1 us
    reduce_scatter x1, waiting for transfers between devices, local(): lax.psum_scatter(jnp.concatenate([query_partial_term, key_term, value_ter...  17.6 us
    psum x1, blocking collectives, by_each_axis(): return lax.psum(partial, second)  17.5 us
    dot_general x2, matrix products, row_contraction(): lax.dot_general(left, right, (((1,), (1,)), ((), ())), preferred_element_...  8.78 us
    dot_general x1, matrix products, local(): jnp.dot(block_of_rows, query_weight, preferred_element_type=jnp.float32)  5.74 us
    dot_general x2, matrix products, token_contraction(): lax.dot_general(left, right, (((0,), (0,)), ((), ())), preferred_element_...  4.2 us
  transfers between devices with their start and end apart: 4, of which 4 were waited for; matrix products, arithmetic and copies ran while one was open for 11% of the time, Pallas kernels for 0%

profile of v1, /device:TPU:0, one launch (start us, length us, event | category | flops | bytes accessed | tf_op | source)
XLA Modules:
  0.0 191.1 jit_solution(12919430982076208088)
XLA Ops:
  7.2 0.0 copy-start
  7.2 0.0 reduce-scatter.3.cloned.1.call-start
  7.2 1.5 copy-done
  8.8 1.7 fusion.58
  10.5 0.1 copy.46
  10.6 1.9 %fusion.17 = bf16[256,128]{1,0:T(8,128)(2,1)S(1)} fusion(bf16[256,4096]{1,0:T(8,128)(2,1)S(1)} %copy-done, bf16[4096,512]{1,0:T(8,128)(2,1)} %param.17, s32[]{:T(128)S(6)} %select_n.18), kind=kOutput, calls=%fused_computation.29 | convolution fusion | flops 268468224 | bytes 3211268 | tf_op jit(solution)/shard_map/dot_general | solution.py:63
  12.5 1.9 %fusion.18 = bf16[256,128]{1,0:T(8,128)(2,1)S(1)} fusion(bf16[256,4096]{1,0:T(8,128)(2,1)S(1)} %copy-done, bf16[4096,512]{1,0:T(8,128)(2,1)} %param.18, s32[]{:T(128)S(6)} %select_n.18), kind=kOutput, calls=%fused_computation.30 | convolution fusion | flops 268468224 | bytes 3211268 | tf_op jit(solution)/shard_map/dot_general | solution.py:64
  14.4 5.7 %fusion.60 = f32[256,1024]{1,0:T(8,128)S(1)} fusion(bf16[256,4096]{1,0:T(8,128)(2,1)S(1)} %copy-done, bf16[4096,1024]{1,0:T(8,128)(2,1)} %param.16), kind=kOutput, calls=%fused_computation.79 | convolution fusion | flops 2147483648 | bytes 11534336 | tf_op jit(solution)/shard_map/dot_general | solution.py:59
  20.2 0.7 fusion.8
  20.9 0.9 pad_maximum_fusion
  21.8 0.0 reduce-scatter.3.cloned.1.call-update
  21.8 0.0 reduce-scatter.5.cloned.1.call-start
  21.9 2.4 %fusion.59 = (bf16[256,32]{0,1:T(8,128)(2,1)S(1)}, f32[256,32]{0,1:T(8,128)S(1)}) fusion(bf16[32,4096]{1,0:T(8,128)(2,1)S(1)} %copy-done.5, bf16[256,4096]{1,0:T(8,128)(2,1)} %param.13, bf16[256]{0:T(256)(128)(2,1)S(1)} %subtract_convert_fusion), kind=kOutput, calls=%fused_computation.78 | convolution fusion | flops 68165632 | bytes 2408960 | tf_op jit(solution)/shard_map/dot_general | solution.py:20
  24.3 0.1 copy.48
  24.5 6.4 %fusion.4 = f32[256,1024]{1,0:T(8,128)S(1)} fusion(bf16[1024,4096]{1,0:T(8,128)(2,1)} %param.19, bf16[256,4096]{1,0:T(8,128)(2,1)} %param.13, bf16[256]{0:T(256)(128)(2,1)S(1)} %subtract_convert_fusion), kind=kOutput, calls=%fused_computation.6 | convolution fusion | flops 2148532224 | bytes 11534848 | tf_op jit(solution)/shard_map/dot_general | solution.py:20
  30.9 0.6 fusion.9
  31.5 0.9 pad_maximum_fusion.1
  32.4 0.0 reduce-scatter.5.cloned.1.call-update
  32.4 0.0 all-reduce.6.cloned.1.call-start
  32.5 0.2 reduce-window.8
  32.7 0.1 convert_reduce_fusion
  32.8 0.1 fusion.44
  32.9 17.6 %reduce-scatter.3.cloned.1.call-done = bf16[64,1312]{1,0:T(8,128)(2,1)} async-done(((bf16[256,1312]{1,0:T(8,128)(2,1)}), bf16[64,1312]{1,0:T(8,128)(2,1)}) %reduce-scatter.3.cloned.1.call-update) | async-done | bytes 167952 | tf_op jit(solution)/shard_map/reduce_scatter | solution.py:65
  50.5 1.2 fusion.41
  51.7 0.9 fusion.14
  52.6 0.1 fusion.31
  52.7 25.9 %reduce-scatter.5.cloned.1.call-done = bf16[64,1056]{1,0:T(8,128)(2,1)} async-done(((bf16[256,1056]{1,0:T(8,128)(2,1)}), bf16[64,1056]{1,0:T(8,128)(2,1)}) %reduce-scatter.5.cloned.1.call-update) | async-done | bytes 135184 | tf_op jit(solution)/shard_map/reduce_scatter | solution.py:101
  78.7 1.2 multiply_reduce_fusion
  79.8 1.1 fusion.10
  81.0 0.3 fusion.25
  81.2 0.3 dynamic_update_slice.7
  81.6 0.0 copy-start.3
  81.6 0.3 dynamic_update_slice.6
  82.0 0.0 copy-start.2
  82.0 0.2 copy-done.3
  82.2 0.4 copy-done.2
  82.6 0.0 all-reduce.6.cloned.1.call-update
  82.6 0.0 all-reduce.8.cloned.1.call-start
  82.7 1.6 fusion.15
  84.3 1.6 fusion.16
  85.8 0.0 all-reduce.8.cloned.1.call-update
  85.9 50.9 %all-reduce.6.cloned.1.call-done = (f32[256,32]{0,1:T(8,128)}, f32[256,32]{0,1:T(8,128)}) async-done(((f32[256,32]{0,1:T(8,128)}, f32[256,32]{0,1:T(8,128)}), (f32[256,32]{0,1:T(8,128)}, f32[256,32]{0,1:T(8,128)})) %all-reduce.6.cloned.1.call-update) | async-done | bytes 65552 | tf_op jit(solution)/shard_map/psum | solution.py:15
  136.7 17.5 %all-reduce.1 = (bf16[256,32]{0,1:T(8,128)(2,1)S(1)}, bf16[256,32]{0,1:T(8,128)(2,1)S(1)}) all-reduce(f32[256,32]{0,1:T(8,128)} %get-tuple-element.4, f32[256,32]{0,1:T(8,128)} %get-tuple-element.5), channel_id=1, replica_groups=mesh['row'=4,'col'=8] {'row'}, use_global_device_ids=true, to_apply=%region_7.8 | all-reduce | flops 16384 | bytes 98304 | tf_op jit(solution)/shard_map/psum | solution.py:16
  154.2 2.9 %convolution_multiply_fusion = f32[32,4096]{1,0:T(8,128)} fusion(bf16[256,4096]{1,0:T(8,128)(2,1)} %param.13, bf16[256]{0:T(256)(128)(2,1)S(1)} %subtract_convert_fusion, bf16[256,32]{0,1:T(8,128)(2,1)S(1)} %get-tuple-element.7), kind=kOutput, calls=%fused_computation | convolution fusion | flops 68288512 | bytes 2638336 | tf_op jit(solution)/shard_map/dot_general | solution.py:26
  157.2 1.3 fusion
  158.4 23.1 %all-reduce.8.cloned.1.call-done = (bf16[32,1024]{1,0:T(8,128)(2,1)}, bf16[1024,32]{0,1:T(8,128)(2,1)}) async-done(((bf16[32,1024]{1,0:T(8,128)(2,1)}, bf16[1024,32]{0,1:T(8,128)(2,1)}), (bf16[32,1024]{1,0:T(8,128)(2,1)}, bf16[1024,32]{0,1:T(8,128)(2,1)})) %all-reduce.8.cloned.1.call-update) | async-done | bytes 131088 | tf_op jit(solution)/shard_map/psum | solution.py:131
  181.5 1.5 convert_element_type.52
  183.0 1.5 convert_element_type.58
  (13 shorter events, 0.0 us)
Async XLA Ops:
  7.2 1.6 copy-start
  7.2 43.3 %reduce-scatter.3.cloned.1.call-start = ((), (), s32[]{:S(2)}) async-start(), calls=%async_computation.2 | async-start | bytes 901120 | tf_op jit(solution)/shard_map/reduce_scatter | solution.py:65
  14.4 5.8 %copy-start.1 = (bf16[32,1024]{1,0:T(8,128)(2,1)S(1)}, bf16[32,1024]{1,0:T(8,128)(2,1)}, u32[]{:S(2)}) copy-start(bf16[32,1024]{1,0:T(8,128)(2,1)} %param.21) | copy-start | bytes 196612
  20.2 1.7 copy-start.6
  20.2 1.7 copy-start.5
  21.8 56.8 %reduce-scatter.5.cloned.1.call-start = ((), (), s32[]{:S(2)}) async-start(), calls=%async_computation.3 | async-start | bytes 737280 | tf_op jit(solution)/shard_map/reduce_scatter | solution.py:101
  24.5 6.4 %copy-start.4 = (bf16[1024,32]{0,1:T(8,128)(2,1)S(1)}, bf16[1024,32]{0,1:T(8,128)(2,1)}, u32[]{:S(2)}) copy-start(bf16[1024,32]{0,1:T(8,128)(2,1)} %param.22) | copy-start | bytes 196612
  30.9 1.6 copy-start.7
  32.4 104.3 %all-reduce.6.cloned.1.call-start = ((), (), s32[]{:S(2)}) async-start(), calls=%async_computation.4 | async-start | bytes 131072 | tf_op jit(solution)/shard_map/psum | solution.py:15
  81.6 0.6 copy-start.3
  82.0 0.6 copy-start.2
  82.6 98.9 %all-reduce.8.cloned.1.call-start = ((), (), s32[]{:S(2)}) async-start(), calls=%async_computation.5 | async-start | bytes 262144 | tf_op jit(solution)/shard_map/psum | solution.py:131
Sparse Core Ops, SparseCore 0:
  22.0 28.4 reduce-scatter.2
  53.6 25.0 reduce-scatter.4
  82.7 53.9 all-reduce.5
  140.3 41.2 all-reduce.7
